TPU v7x, 32 devices: a whole 2x2x4 slice. The times are simulated.
32 devices in a mesh: tile: 8 (over z, y), chan: 4 (over x, core).
Axes of the slice: x: 2, y: 2, z: 4, core: 2. Of those that a mesh axis runs over, the one named last changes fastest.
Arguments:
- feat: bfloat16 [128, 64, 256], P('tile', 'chan'), may hold values from -6 to 6
- lift: float32 [64], replicated, may hold values from -3 to 3
- dilation4_weight: bfloat16 [3, 3, 64, 64], replicated, may hold values from -0.25 to 0.25
- dilation8_weight: bfloat16 [3, 3, 64, 64], replicated, may hold values from -0.25 to 0.25
- entry_fraction: bfloat16 [2048, 128], P('tile'), may hold values from 0.019897461 to 0.19921875
- entry_target_tile: int32 [2048, 1], P('tile'), may hold values from 0 to 7; in each aligned block of 256 rows (0 to 255, 256 to 511, ...) at most 64 rows name the same one
- entry_owner_tile: int32 [2048], P('tile'), may hold values from 0 to 31
- entry_local_net: int32 [2048], P('tile'), may hold values from 0 to 63
- pin_demand_weight: float32 [2048], P('tile'), may hold values from 0.2 to 2
- pin_local_net: int32 [2048], P('tile'), may hold values from 0 to 63
- pin_global_cell: int32 [2048], P('tile'), may hold values from 0 to 511
Outputs:
- cell_grad: float32 [512], P('tile')
Inputs may be any that keep to these rules, and one draw needn't show every extreme that they name: `entry_target_tile`: among the entries of one tile index, at most 64 name the same destination, and in some tile index exactly 64 do.
All inputs are finite; a program needn't handle non-finite values.
Results may differ from a plain program's by a relative error of at most 0.0003.
Values may be sent and summed in bfloat16 or wider, within the bound.
A program may use at most 64 MiB of HBM per device.

v0:
```python
import jax
import jax.numpy as jnp
from jax import lax
from jax.sharding import PartitionSpec as P

NET_DEV = 64
CELL_DEV = 64
TILE_DEV = 32


def extended(array, sides, width):
    for axis, dim in sides:
        peers, length = (lax.axis_size(axis), array.shape[dim])
        up = [(i, (i + 1) % peers) for i in range(peers - 1)]
        down = [(j, i) for i, j in up]
        last = lax.slice_in_dim(array, length - width, length, axis=dim)
        leading = lax.slice_in_dim(array, 0, width, axis=dim)
        before = lax.ppermute(last, axis, up)
        after = lax.ppermute(leading, axis, down)
        array = jnp.concatenate([before, array, after], axis=dim)
    return array


def flipped_kernel(kernel):
    return jnp.transpose(kernel[::-1, ::-1], (0, 1, 3, 2))


def dilated_convolution(own_part, weights, channel_start, dilation):
    row_count, chan_own, col_count = own_part.shape
    rimmed = extended(own_part, (("tile", 0),), dilation)
    own_weights = lax.dynamic_slice_in_dim(weights, channel_start, chan_own, 3)
    start_sum = jnp.zeros((row_count, chan_own, col_count), jnp.float32)
    running = start_sum
    widened = jnp.pad(
        lax.all_gather(rimmed, "chan", axis=1, tiled=True), ((0, 0), (0, 0), (dilation, dilation))
    )
    for row_tap in range(3):
        for col_tap in range(3):
            part_in = widened[
                row_tap * dilation : row_tap * dilation + row_count,
                :,
                col_tap * dilation : col_tap * dilation + col_count,
            ]
            running = running + jnp.einsum(
                "rcw,co->row",
                part_in,
                own_weights[row_tap, col_tap],
                preferred_element_type=jnp.float32,
            )
    return running


def local(
    feat,
    lift,
    dilation4_weight,
    dilation8_weight,
    entry_fraction,
    entry_target_tile,
    entry_owner_tile,
    entry_local_net,
    pin_demand_weight,
    pin_local_net,
    pin_global_cell,
):
    highest = lax.Precision.HIGHEST
    tile_count = lax.axis_size("tile")
    chan_count = lax.axis_size("chan")
    row_count, chan_own, col_count = feat.shape
    channel_start = lax.axis_index("chan") * chan_own
    lift_own = lax.dynamic_slice_in_dim(lift, channel_start, chan_own, 0)
    entry_count = entry_target_tile.shape[0]
    capacity = chan_count * max(1, 2 * entry_count // (chan_count * tile_count))
    part_total = 1
    part_id = 0
    slot_count = capacity // part_total
    destination = entry_target_tile[:, 0]
    dest_hot = (destination[:, None] == jnp.arange(tile_count, dtype=jnp.int32)[None, :]).astype(
        jnp.int32
    )
    rank = jnp.sum(jnp.cumsum(dest_hot, axis=0) * dest_hot, axis=1) - 1
    placed = rank % part_total == part_id
    slot_row = jnp.where(
        placed, destination * slot_count + rank // part_total, tile_count * slot_count
    )
    pin_hot = (pin_local_net[None, :] == jnp.arange(NET_DEV, dtype=jnp.int32)[:, None]).astype(
        jnp.float32
    )
    strength = jnp.dot(pin_hot, pin_demand_weight, precision=highest)
    entry_hot = (entry_local_net[:, None] == jnp.arange(NET_DEV, dtype=jnp.int32)[None, :]).astype(
        jnp.float32
    )
    entry_strength = jnp.dot(entry_hot, strength, precision=highest)
    frac = entry_fraction.astype(jnp.float32)
    payload = entry_strength[:, None] * frac
    send_rows = (
        jnp.zeros((tile_count * slot_count, 128), jnp.float32)
        .at[slot_row]
        .set(payload, mode="drop")
    )
    send_ids = (
        jnp.zeros((tile_count * slot_count,), jnp.int32)
        .at[slot_row]
        .set(entry_owner_tile, mode="drop")
    )
    arrived, arrived_ids = (
        lax.all_to_all(
            send_rows.reshape(tile_count, slot_count, 128).astype(jnp.bfloat16),
            "tile",
            split_axis=0,
            concat_axis=0,
            tiled=True,
        ).astype(jnp.float32),
        lax.all_to_all(
            send_ids.reshape(tile_count, slot_count),
            "tile",
            split_axis=0,
            concat_axis=0,
            tiled=True,
        ),
    )
    tile_hot = (
        arrived_ids.reshape(-1)[:, None] == jnp.arange(TILE_DEV, dtype=jnp.int32)[None, :]
    ).astype(jnp.float32)
    tiles = jnp.dot(tile_hot.T, arrived.reshape(-1, 128), precision=highest)
    demand = (
        tiles.reshape(row_count // 8, col_count // 16, 8, 16)
        .transpose(0, 2, 1, 3)
        .reshape(row_count, col_count)
    )
    input_features = (
        feat.astype(jnp.float32) + demand[:, None, :] * lift_own[None, :, None]
    ).astype(jnp.bfloat16)
    first_preactivation = dilated_convolution(input_features, dilation4_weight, channel_start, 4)
    hidden_features = jax.nn.silu(first_preactivation).astype(jnp.bfloat16)
    second_output = dilated_convolution(hidden_features, dilation8_weight, channel_start, 8)
    second_gradient = jax.nn.sigmoid(second_output).astype(jnp.bfloat16)
    hidden_gradient = dilated_convolution(
        second_gradient, flipped_kernel(dilation8_weight), channel_start, 8
    )
    sigmoid_pre = jax.nn.sigmoid(first_preactivation)
    preactivation_gradient = (
        hidden_gradient * sigmoid_pre * (1.0 + first_preactivation * (1.0 - sigmoid_pre))
    ).astype(jnp.bfloat16)
    inputs_gradient = dilated_convolution(
        preactivation_gradient, flipped_kernel(dilation4_weight), channel_start, 4
    )
    partial_grad = jnp.sum(inputs_gradient * lift_own[None, :, None], axis=1)
    grad_demand = lax.psum(partial_grad, "chan")
    grad_tiles = (
        grad_demand.reshape(row_count // 8, 8, col_count // 16, 16)
        .transpose(0, 2, 1, 3)
        .reshape(TILE_DEV, 128)
    )
    slot_grads = jnp.dot(tile_hot, grad_tiles, precision=highest).reshape(
        tile_count, slot_count, 128
    )
    returned = lax.all_to_all(
        slot_grads.astype(jnp.bfloat16), "tile", split_axis=0, concat_axis=0, tiled=True
    ).astype(slot_grads.dtype)
    entry_rows = jnp.take(returned.reshape(-1, 128), slot_row, axis=0, mode="fill", fill_value=0.0)
    entry_grad = jnp.sum(entry_rows * frac, axis=1)
    grad_net = jnp.dot(entry_grad, entry_hot, precision=highest)
    pin_grad = jnp.dot(grad_net, pin_hot, precision=highest)
    cell_term = jax.ops.segment_sum(pin_grad, pin_global_cell, num_segments=CELL_DEV * tile_count)
    return lax.psum_scatter(cell_term, "tile", scatter_dimension=0, tiled=True)


def solution(mesh):
    in_specs = (
        P("tile", "chan", None),
        P(),
        P(),
        P(),
        P("tile", None),
        P("tile", None),
        P("tile"),
        P("tile"),
        P("tile"),
        P("tile"),
        P("tile"),
    )
    out_specs = P("tile")
    return jax.shard_map(local, mesh=mesh, in_specs=in_specs, out_specs=out_specs, check_vma=False)
```

profile of v0, /device:TPU:0, one launch (start us, length us, event | category | flops | bytes accessed | tf_op | source)
XLA Modules:
  0.0 194.8 jit_solution(14243430125302070767)
XLA Ops:
  6.5 0.7 fusion.60
  7.3 0.6 reduce-window.6
  8.1 0.8 fusion.59
  8.9 0.7 and_reduce_fusion
  9.6 1.6 scatter_custom_fusion
  11.1 0.7 all_to_all.12
  11.8 7.3 %all-to-all-start = ((s32[8,1,64]{2,1,0:T(1,128)}), s32[8,1,64]{2,1,0:T(1,128)S(1)}, u32[]{:S(2)}, u32[]{:S(2)}) async-start(s32[8,1,64]{2,1,0:T(1,128)} %all_to_all.12), calls=%async_computation | async-start | bytes 8192 | tf_op jit(solution)/shard_map/all_to_all | solution.py:114
  19.1 0.8 convolution_bitcast_fusion.2
  19.9 0.9 fusion.42
  20.8 1.7 scatter_custom_fusion.1
  22.5 0.7 convert_element_type.46
  23.2 2.4 %all-to-all-done = s32[8,1,64]{2,1,0:T(1,128)S(1)} async-done(((s32[8,1,64]{2,1,0:T(1,128)}), s32[8,1,64]{2,1,0:T(1,128)S(1)}, u32[]{:S(2)}, u32[]{:S(2)}) %all-to-all-start) | async-done | bytes 2080 | tf_op jit(solution)/shard_map/all_to_all | solution.py:114
  25.6 3.6 %all-to-all-start.1 = ((bf16[8,64,128]{2,1,0:T(8,128)(2,1)}), bf16[8,64,128]{2,1,0:T(8,128)(2,1)S(1)}, u32[]{:S(2)}, u32[]{:S(2)}) async-start(bf16[8,64,128]{2,1,0:T(8,128)(2,1)} %bitcast.24), calls=%async_computation.1 | async-start | bytes 262144 | tf_op jit(solution)/shard_map/all_to_all | solution.py:107
  29.3 0.5 broadcast.170
  29.8 0.7 reduce.8
  30.5 5.9 %all-to-all-done.1 = bf16[8,64,128]{2,1,0:T(8,128)(2,1)S(1)} async-done(((bf16[8,64,128]{2,1,0:T(8,128)(2,1)}), bf16[8,64,128]{2,1,0:T(8,128)(2,1)S(1)}, u32[]{:S(2)}, u32[]{:S(2)}) %all-to-all-start.1) | async-done | bytes 131104 | tf_op jit(solution)/shard_map/all_to_all | solution.py:107
  37.2 1.3 collective-permute-start.1
  38.5 4.5 %collective-permute-start = (bf16[4,16,256]{2,1,0:T(8,128)(2,1)S(1)}, bf16[4,16,256]{2,1,0:T(8,128)(2,1)S(1)}, u32[]{:S(2)}, u32[]{:S(2)}) collective-permute-start(bf16[4,16,256]{2,1,0:T(8,128)(2,1)S(1)} %get-tuple-element.13), channel_id=1, source_target_pairs={{0,4},{4,8},{8,12},{12,16},{16,20},{20,24},{24,28},{1,5},{5,9},{9,... | collective-permute-start | bytes 98312 | tf_op jit(solution)/shard_map/ppermute | solution.py:18
  43.1 1.6 collective-permute-done
  44.7 8.6 %all_gather.12 = bf16[24,64,256]{2,1,0:T(8,128)(2,1)S(1)} all-gather(bf16[24,16,256]{2,1,0:T(8,128)(2,1)S(1)} %pad_maximum_fusion.2), channel_id=1, replica_groups=mesh['tile'=8,'chan'=4] {'chan'}, dimensions={1}, use_global_device_ids=true | all-gather | bytes 983040 | tf_op jit(solution)/shard_map/all_gather | solution.py:35
  56.0 0.4 multiply_convert_fusion
  56.4 1.3 collective-permute-start.3
  57.7 4.9 %collective-permute-start.2 = (bf16[8,16,256]{2,1,0:T(8,128)(2,1)S(1)}, bf16[8,16,256]{2,1,0:T(8,128)(2,1)S(1)}, u32[]{:S(2)}, u32[]{:S(2)}) collective-permute-start(bf16[8,16,256]{2,1,0:T(8,128)(2,1)S(1)} %get-tuple-element.11), channel_id=1, source_target_pairs={{0,4},{4,8},{8,12},{12,16},{16,20},{20,24},{24,28},{1,5},{5,9},{9,... | collective-permute-start | bytes 196616 | tf_op jit(solution)/shard_map/ppermute | solution.py:18
  62.6 0.7 collective-permute-done.3
  63.2 1.6 collective-permute-done.2
  64.8 0.8 pad_maximum_fusion
  65.6 17.1 %all-gather.3.cloned.1.call-done = bf16[32,64,256]{2,1,0:T(8,128)(2,1)} async-done(((bf16[32,16,256]{2,1,0:T(8,128)(2,1)}), bf16[32,64,256]{2,1,0:T(8,128)(2,1)}) %all-gather.3.cloned.1.call-update) | async-done | bytes 1048592 | tf_op jit(solution)/shard_map/all_gather | solution.py:35
  82.7 1.5 fusion.33
  86.9 1.6 fusion.46
  88.6 1.3 collective-permute-start.5
  89.9 4.7 %collective-permute-start.4 = (bf16[8,16,256]{2,0,1:T(8,128)(2,1)S(1)}, bf16[8,16,256]{2,0,1:T(8,128)(2,1)S(1)}, u32[]{:S(2)}, u32[]{:S(2)}) collective-permute-start(bf16[8,16,256]{2,0,1:T(8,128)(2,1)S(1)} %get-tuple-element.9), channel_id=1, source_target_pairs={{0,4},{4,8},{8,12},{12,16},{16,20},{20,24},{24,28},{1,5},{5,9},{9,... | collective-permute-start | bytes 196616 | tf_op jit(solution)/shard_map/ppermute | solution.py:18
  94.7 1.6 collective-permute-done.4
  96.3 0.7 pad_maximum_fusion.1
  97.2 18.6 %all-gather.5.cloned.1.call-done = bf16[32,64,256]{2,0,1:T(8,128)(2,1)} async-done(((bf16[32,16,256]{2,0,1:T(8,128)(2,1)}), bf16[32,64,256]{2,0,1:T(8,128)(2,1)}) %all-gather.5.cloned.1.call-update) | async-done | bytes 1048592 | tf_op jit(solution)/shard_map/all_gather | solution.py:35
  115.7 1.8 copy.66
  120.1 1.3 collective-permute-start.7
  121.4 4.5 %collective-permute-start.6 = (bf16[4,16,256]{2,1,0:T(8,128)(2,1)S(1)}, bf16[4,16,256]{2,1,0:T(8,128)(2,1)S(1)}, u32[]{:S(2)}, u32[]{:S(2)}) collective-permute-start(bf16[4,16,256]{2,1,0:T(8,128)(2,1)S(1)} %get-tuple-element.7), channel_id=1, source_target_pairs={{0,4},{4,8},{8,12},{12,16},{16,20},{20,24},{24,28},{1,5},{5,9},{9,... | collective-permute-start | bytes 98312 | tf_op jit(solution)/shard_map/ppermute | solution.py:18
  126.0 1.5 collective-permute-done.6
  127.6 7.5 %all_gather.15 = bf16[24,64,256]{2,1,0:T(8,128)(2,1)S(1)} all-gather(bf16[24,16,256]{2,1,0:T(8,128)(2,1)S(1)} %pad_maximum_fusion.3), channel_id=1, replica_groups=mesh['tile'=8,'chan'=4] {'chan'}, dimensions={1}, use_global_device_ids=true | all-gather | bytes 983040 | tf_op jit(solution)/shard_map/all_gather | solution.py:35
  137.8 11.7 %psum.7 = f32[32,128]{1,0:T(8,128)S(1)} all-reduce(f32[32,128]{1,0:T(8,128)S(1)} %reshape.105), channel_id=1, replica_groups=mesh['tile'=8,'chan'=4] {'chan'}, use_global_device_ids=true, to_apply=%region_6.7 | all-reduce | flops 4096 | bytes 32768 | tf_op jit(solution)/shard_map/psum | solution.py:149
  149.6 1.0 convolution_convert_fusion
  150.6 7.4 %all-to-all-start.2 = ((bf16[8,64,128]{2,1,0:T(8,128)(2,1)}), bf16[8,64,128]{2,1,0:T(8,128)(2,1)S(1)}, u32[]{:S(2)}, u32[]{:S(2)}) async-start(bf16[8,64,128]{2,1,0:T(8,128)(2,1)} %convolution_convert_fusion), calls=%async_computation.2 | async-start | bytes 262144 | tf_op jit(solution)/shard_map/all_to_all | solution.py:158
  158.0 0.6 dynamic-slice.8
  159.3 6.1 %all-to-all-done.2 = bf16[8,64,128]{2,1,0:T(8,128)(2,1)S(1)} async-done(((bf16[8,64,128]{2,1,0:T(8,128)(2,1)}), bf16[8,64,128]{2,1,0:T(8,128)(2,1)S(1)}, u32[]{:S(2)}, u32[]{:S(2)}) %all-to-all-start.2) | async-done | bytes 131104 | tf_op jit(solution)/shard_map/all_to_all | solution.py:158
  165.4 0.7 gather_fusion
  166.7 2.5 %scatter_custom_fusion.2 = f32[512]{0:T(512)S(1)} fusion(s32[256]{0:T(256)} %param.21, f32[256]{0:T(256)S(1)} %bitcast.284, f32[]{:T(128)} %constant.62.clone.1), kind=kCustom, calls=%fused_computation.201 | custom fusion | flops 256 | bytes 2560 | tf_op jit(solution)/shard_map/scatter-add | solution.py:165
  169.2 18.2 %all-reduce.4 = f32[512]{0:T(512)S(1)} all-reduce(f32[512]{0:T(512)S(1)} %scatter_custom_fusion.2), channel_id=2, replica_groups=mesh['tile'=8,'chan'=4] {'tile'}, use_global_device_ids=true, to_apply=%region_9.10.clone | all-reduce | flops 512 | bytes 4096
  187.4 0.6 dynamic-slice.9
  (90 shorter events, 12.8 us)
Async XLA Ops:
  6.5 12.6 %copy-start = (f32[256]{0:T(256)S(1)}, f32[256]{0:T(256)}, u32[]{:S(2)}) copy-start(f32[256]{0:T(256)} %param.19) | copy-start | bytes 3076
  6.5 22.7 %copy-start.8 = (f32[64]{0:T(128)S(1)}, f32[64]{0:T(128)}, u32[]{:S(2)}) copy-start(f32[64]{0:T(128)} %param.12) | copy-start | bytes 772
  6.5 30.5 %copy-start.5 = (bf16[16,16,256]{2,1,0:T(8,128)(2,1)S(1)}, bf16[16,16,256]{2,1,0:T(8,128)(2,1)}, u32[]{:S(2)}) copy-start(bf16[16,16,256]{2,1,0:T(8,128)(2,1)} %param.11) | copy-start | bytes 393220
  11.8 13.8 %all-to-all-start = ((s32[8,1,64]{2,1,0:T(1,128)}), s32[8,1,64]{2,1,0:T(1,128)S(1)}, u32[]{:S(2)}, u32[]{:S(2)}) async-start(s32[8,1,64]{2,1,0:T(1,128)} %all_to_all.12), calls=%async_computation | async-start | bytes 8192 | tf_op jit(solution)/shard_map/all_to_all | solution.py:114
  25.6 10.9 %all-to-all-start.1 = ((bf16[8,64,128]{2,1,0:T(8,128)(2,1)}), bf16[8,64,128]{2,1,0:T(8,128)(2,1)S(1)}, u32[]{:S(2)}, u32[]{:S(2)}) async-start(bf16[8,64,128]{2,1,0:T(8,128)(2,1)} %bitcast.24), calls=%async_computation.1 | async-start | bytes 262144 | tf_op jit(solution)/shard_map/all_to_all | solution.py:107
  29.2 53.6 %all-gather.3.cloned.1.call-start = ((), (), s32[]{:S(2)}) async-start(), calls=%async_computation.3 | async-start | bytes 1310720 | tf_op jit(solution)/shard_map/all_gather | solution.py:35
  36.6 16.7 %copy-start.3 = (bf16[3,3,64,64]{3,2,1,0:T(8,128)(2,1)S(1)}, bf16[3,3,64,64]{3,2,1,0:T(8,128)(2,1)}, u32[]{:S(2)}) copy-start(bf16[3,3,64,64]{3,2,1,0:T(8,128)(2,1)} %param.13) | copy-start | bytes 221188
  37.2 5.9 %collective-permute-start.1 = (bf16[4,16,256]{2,1,0:T(8,128)(2,1)S(1)}, bf16[4,16,256]{2,1,0:T(8,128)(2,1)S(1)}, u32[]{:S(2)}, u32[]{:S(2)}) collective-permute-start(bf16[4,16,256]{2,1,0:T(8,128)(2,1)S(1)} %get-tuple-element.14), channel_id=1, source_target_pairs={{4,0},{8,4},{12,8},{16,12},{20,16},{24,20},{28,24},{5,1},{9,5},{13... | collective-permute-start | bytes 98312 | tf_op jit(solution)/shard_map/ppermute | solution.py:19
  38.5 6.1 %collective-permute-start = (bf16[4,16,256]{2,1,0:T(8,128)(2,1)S(1)}, bf16[4,16,256]{2,1,0:T(8,128)(2,1)S(1)}, u32[]{:S(2)}, u32[]{:S(2)}) collective-permute-start(bf16[4,16,256]{2,1,0:T(8,128)(2,1)S(1)} %get-tuple-element.13), channel_id=1, source_target_pairs={{0,4},{4,8},{8,12},{12,16},{16,20},{20,24},{24,28},{1,5},{5,9},{9,... | collective-permute-start | bytes 98312 | tf_op jit(solution)/shard_map/ppermute | solution.py:18
  56.0 26.7 %copy-start.2 = (bf16[3,3,64,64]{3,2,1,0:T(8,128)(2,1)S(1)}, bf16[3,3,64,64]{3,2,1,0:T(8,128)(2,1)}, u32[]{:S(2)}) copy-start(bf16[3,3,64,64]{3,2,1,0:T(8,128)(2,1)} %param.14) | copy-start | bytes 221188
  56.4 6.8 %collective-permute-start.3 = (bf16[8,16,256]{2,1,0:T(8,128)(2,1)S(1)}, bf16[8,16,256]{2,1,0:T(8,128)(2,1)S(1)}, u32[]{:S(2)}, u32[]{:S(2)}) collective-permute-start(bf16[8,16,256]{2,1,0:T(8,128)(2,1)S(1)} %get-tuple-element.12), channel_id=1, source_target_pairs={{4,0},{8,4},{12,8},{16,12},{20,16},{24,20},{28,24},{5,1},{9,5},{13... | collective-permute-start | bytes 196616 | tf_op jit(solution)/shard_map/ppermute | solution.py:19
  57.7 7.1 %collective-permute-start.2 = (bf16[8,16,256]{2,1,0:T(8,128)(2,1)S(1)}, bf16[8,16,256]{2,1,0:T(8,128)(2,1)S(1)}, u32[]{:S(2)}, u32[]{:S(2)}) collective-permute-start(bf16[8,16,256]{2,1,0:T(8,128)(2,1)S(1)} %get-tuple-element.11), channel_id=1, source_target_pairs={{0,4},{4,8},{8,12},{12,16},{16,20},{20,24},{24,28},{1,5},{5,9},{9,... | collective-permute-start | bytes 196616 | tf_op jit(solution)/shard_map/ppermute | solution.py:18
  65.6 50.2 %all-gather.5.cloned.1.call-start = ((), (), s32[]{:S(2)}) async-start(), calls=%async_computation.4 | async-start | bytes 1310720 | tf_op jit(solution)/shard_map/all_gather | solution.py:35
  82.7 1.5 copy-start.1
  88.6 6.2 %collective-permute-start.5 = (bf16[8,16,256]{2,0,1:T(8,128)(2,1)S(1)}, bf16[8,16,256]{2,0,1:T(8,128)(2,1)S(1)}, u32[]{:S(2)}, u32[]{:S(2)}) collective-permute-start(bf16[8,16,256]{2,0,1:T(8,128)(2,1)S(1)} %get-tuple-element.10), channel_id=1, source_target_pairs={{4,0},{8,4},{12,8},{16,12},{20,16},{24,20},{28,24},{5,1},{9,5},{13... | collective-permute-start | bytes 196616 | tf_op jit(solution)/shard_map/ppermute | solution.py:19
  89.9 6.4 %collective-permute-start.4 = (bf16[8,16,256]{2,0,1:T(8,128)(2,1)S(1)}, bf16[8,16,256]{2,0,1:T(8,128)(2,1)S(1)}, u32[]{:S(2)}, u32[]{:S(2)}) collective-permute-start(bf16[8,16,256]{2,0,1:T(8,128)(2,1)S(1)} %get-tuple-element.9), channel_id=1, source_target_pairs={{0,4},{4,8},{8,12},{12,16},{16,20},{20,24},{24,28},{1,5},{5,9},{9,... | collective-permute-start | bytes 196616 | tf_op jit(solution)/shard_map/ppermute | solution.py:18
  120.1 5.9 %collective-permute-start.7 = (bf16[4,16,256]{2,1,0:T(8,128)(2,1)S(1)}, bf16[4,16,256]{2,1,0:T(8,128)(2,1)S(1)}, u32[]{:S(2)}, u32[]{:S(2)}) collective-permute-start(bf16[4,16,256]{2,1,0:T(8,128)(2,1)S(1)} %get-tuple-element.8), channel_id=1, source_target_pairs={{4,0},{8,4},{12,8},{16,12},{20,16},{24,20},{28,24},{5,1},{9,5},{13... | collective-permute-start | bytes 98312 | tf_op jit(solution)/shard_map/ppermute | solution.py:19
  121.4 6.1 %collective-permute-start.6 = (bf16[4,16,256]{2,1,0:T(8,128)(2,1)S(1)}, bf16[4,16,256]{2,1,0:T(8,128)(2,1)S(1)}, u32[]{:S(2)}, u32[]{:S(2)}) collective-permute-start(bf16[4,16,256]{2,1,0:T(8,128)(2,1)S(1)} %get-tuple-element.7), channel_id=1, source_target_pairs={{0,4},{4,8},{8,12},{12,16},{16,20},{20,24},{24,28},{1,5},{5,9},{9,... | collective-permute-start | bytes 98312 | tf_op jit(solution)/shard_map/ppermute | solution.py:18
  137.2 20.8 %copy-start.9 = (u32[32]{0:T(128)S(1)}, u32[32]{0:T(128)}, u32[]{:S(2)}) copy-start(u32[32]{0:T(128)} %constant.82) | copy-start | bytes 388
  137.8 28.3 %copy-start.4 = (bf16[256,128]{1,0:T(8,128)(2,1)S(1)}, bf16[256,128]{1,0:T(8,128)(2,1)}, u32[]{:S(2)}) copy-start(bf16[256,128]{1,0:T(8,128)(2,1)} %param.15) | copy-start | bytes 196612
  150.6 15.7 %copy-start.6 = (s32[256]{0:T(256)S(1)}, s32[256]{0:T(256)}, u32[]{:S(2)}) copy-start(s32[256]{0:T(256)} %param.18) | copy-start | bytes 3076
  150.6 15.9 %copy-start.7 = (s32[256]{0:T(256)S(1)}, s32[256]{0:T(256)}, u32[]{:S(2)}) copy-start(s32[256]{0:T(256)} %param.20) | copy-start | bytes 3076
  150.6 14.7 %all-to-all-start.2 = ((bf16[8,64,128]{2,1,0:T(8,128)(2,1)}), bf16[8,64,128]{2,1,0:T(8,128)(2,1)S(1)}, u32[]{:S(2)}, u32[]{:S(2)}) async-start(bf16[8,64,128]{2,1,0:T(8,128)(2,1)} %convolution_convert_fusion), calls=%async_computation.2 | async-start | bytes 262144 | tf_op jit(solution)/shard_map/all_to_all | solution.py:158
Sparse Core Ops, SparseCore 0:
  65.7 16.9 all-gather.2
  97.2 18.4 all-gather.4
where the time goes:
time: 196 us; the launch traced here: 195 us
  waiting for transfers between devices  57.2 us (29%)
  blocking collectives  46 us (23%)
  starting transfers between devices  42.2 us (22%)
  matrix products  15.8 us (8%)
  between operations  14.4 us (7%)
  other arithmetic  11.8 us (6%)
  local copies, waits for them, and re-layouts  7.41 us (4%)
    all_gather x2, waiting for transfers between devices, dilated_convolution(): lax.all_gather(rimmed, 'chan', axis=1, tiled=True)  35.7 us
    ppermute x4, starting transfers between devices, extended(): before = lax.ppermute(last, axis, up)  18.7 us
    unnamed x1, blocking collectives  18.2 us
    all_gather x2, blocking collectives, dilated_convolution(): lax.all_gather(rimmed, 'chan', axis=1, tiled=True)  16.1 us
    dot_general x36, matrix products, dilated_convolution(): jnp.einsum('rcw,co->row', part_in, own_weights[row_tap, col_tap], preferr...  12.4 us
    psum x1, blocking collectives, local(): grad_demand = lax.psum(partial_grad, 'chan')  11.7 us
    all_to_all x1, starting transfers between devices, local(): lax.all_to_all(slot_grads.astype(jnp.bfloat16), 'tile', split_axis=0, con...  7.38 us
    all_to_all x1, starting transfers between devices, local(): lax.all_to_all(send_ids.reshape(tile_count, slot_count), 'tile', split_ax...  7.31 us
  transfers between devices with their start and end apart: 13, of which 11 were waited for; matrix products, arithmetic and copies ran while one was open for 3% of the time, Pallas kernels for 0%

commit v1 on v0

v1 whole, which is shorter than its diff:
```python
import functools

import jax
import jax.numpy as jnp
from jax import lax
from jax.experimental import pallas as pl
from jax.experimental.pallas import tpu as pltpu
from jax.sharding import PartitionSpec as P

MESH = pl.DeviceIdType.MESH
CELL_DEV = 64
TILE_ROWS = 8
TILE_COLS = 16
LANES = 128
HALO = 24
GROUP = 4
F32 = jnp.float32
BF16 = jnp.bfloat16


def split(x, terms):
    parts = []
    for _ in range(terms):
        part = x.astype(BF16)
        parts.append(part)
        x = x - part.astype(F32)
    return parts


def kernel(
    tiles, chans,
    feat, lift, w4, w8, frac, pack,
    out,
    win, gath, inp, pre, hid, sec, gpre, wm1, wm2, wm3, wm4,
    fmask, dbuf, dsend, drecv, demand, gown, gall, csend, crecv,
    fsend_sem, frecv_sem, own_sem, dsend_sem, drecv_sem, gsend_sem, grecv_sem, gown_sem,
    csend_sem, crecv_sem,
):
    ti = lax.axis_index("tile")
    ci = lax.axis_index("chan")
    rows, chan_own, cols = feat.shape
    chan = chan_own * chans
    own_cols = cols // chans
    margin = (LANES - own_cols) // 2
    reach = -(-HALO // rows)
    in_rows = rows + 2 * HALO
    others = tiles * chans - 1

    barrier = pltpu.get_barrier_semaphore()

    def peer(step):
        number = lax.rem(ti * chans + ci + step, tiles * chans)
        return lax.div(number, chans), lax.rem(number, chans)

    def greet(step, carry):
        pl.semaphore_signal(barrier, inc=1, device_id=peer(step), device_id_type=MESH)
        return carry

    lax.fori_loop(1, others + 1, greet, 0)

    flat = feat[...].astype(F32).reshape(rows * chan_own, cols)
    lane = lax.broadcasted_iota(jnp.int32, (1, LANES), 1)
    for k in range(chans):
        first = k * own_cols - margin
        turned = pltpu.roll(flat, (-first) % cols, 1)[:, :LANES]
        inside = (lane + first >= 0) & (lane + first < cols)
        win[k] = jnp.where(inside, turned, 0.0).astype(BF16).reshape(rows, chan_own, LANES)

    pl.semaphore_wait(barrier, others)

    def spans(delta):
        start = HALO - rows * delta
        low = max(0, -start)
        high = min(rows, in_rows - start)
        return low, high - low, start + low

    def feat_copy(delta, k):
        low, count, at = spans(delta)
        to = lax.rem(ci + k, chans)
        src = win.at[to, pl.ds(low, count)]
        dst = gath.at[pl.ds(at, count), pl.ds(pl.multiple_of(ci * chan_own, chan_own), chan_own)]
        if delta == 0 and k == 0:
            return pltpu.make_async_copy(src, dst, own_sem)
        return pltpu.make_async_remote_copy(
            src_ref=src, dst_ref=dst,
            send_sem=fsend_sem.at[delta + reach, k], recv_sem=frecv_sem.at[delta + reach, k],
            device_id=(ti + delta, to), device_id_type=MESH,
        )

    def feat_arrival(delta, k):
        low, count, at = spans(delta)
        come = lax.rem(ci + chans - k, chans)
        dst = gath.at[pl.ds(at, count), pl.ds(pl.multiple_of(come * chan_own, chan_own), chan_own)]
        return pltpu.make_async_remote_copy(
            src_ref=dst, dst_ref=dst,
            send_sem=fsend_sem.at[delta + reach, k], recv_sem=frecv_sem.at[delta + reach, k],
            device_id=(ti, lax.rem(ci + 1, chans)), device_id_type=MESH,
        )

    order = [(d, k) for d in sorted(range(-reach, reach + 1), key=lambda d: -abs(d)) for k in range(chans)]
    for delta, k in order:
        if delta == 0:
            feat_copy(delta, k).start()
        else:
            @pl.when((ti + delta >= 0) & (ti + delta < tiles))
            def _(delta=delta, k=k):
                feat_copy(delta, k).start()

    table = pack[...]
    columns = jnp.transpose(table)
    entries = table.shape[1]
    net_e_col, wpin_col, net_p_col = columns[:, 2:3], columns[:, 3:4], columns[:, 4:5]
    strength = jnp.sum(
        jnp.where(net_p_col == table[2:3, :], wpin_col, 0.0), axis=0, keepdims=True
    )
    src_j = lax.broadcasted_iota(jnp.int32, (LANES, TILE_ROWS * LANES), 0)
    dst_j = lax.broadcasted_iota(jnp.int32, (LANES, TILE_ROWS * LANES), 1)
    pick = src_j == (dst_j // LANES) * TILE_COLS + dst_j % TILE_COLS
    spread = jnp.dot(
        frac[...], jnp.where(pick, 1.0, 0.0).astype(BF16), preferred_element_type=F32
    )
    wide = lax.broadcasted_iota(jnp.int32, (1, TILE_ROWS * LANES), 1) % LANES
    block = (wide + ci * own_cols - margin + TILE_COLS * LANES) // TILE_COLS - LANES
    fmask[...] = jnp.where(columns[:, 1:2] == block.astype(F32), spread, 0.0).astype(BF16)
    pad_blocks = HALO // TILE_ROWS
    blocks = dbuf.shape[0] // TILE_ROWS
    block_row = lax.broadcasted_iota(jnp.int32, (blocks, entries), 0).astype(F32)
    placed = jnp.where(block_row == table[0:1, :] + float(pad_blocks), strength, 0.0)
    left = jnp.concatenate(split(placed, 2), axis=0)
    partial = jnp.dot(left, fmask[...], preferred_element_type=F32)
    partial = partial[:blocks] + partial[blocks:]
    for i in range(TILE_ROWS):
        dbuf[pl.ds(i, blocks, stride=TILE_ROWS), :] = partial[:, i * LANES : (i + 1) * LANES]
    dsend[...] = dbuf[...].astype(BF16)

    def demand_copy(step):
        to = lax.rem(ti + step, tiles)
        return pltpu.make_async_remote_copy(
            src_ref=dsend.at[pl.ds(pl.multiple_of(to * rows, rows), in_rows)],
            dst_ref=drecv.at[step],
            send_sem=dsend_sem.at[step], recv_sem=drecv_sem.at[step],
            device_id=(to, ci), device_id_type=MESH,
        )

    def each(lo, hi, fn):
        def body(step, carry):
            fn(step)
            return carry
        lax.fori_loop(lo, hi, body, 0)

    each(1, tiles, lambda s: demand_copy(s).start())

    lift_row = lift[...]
    lift_col = jnp.transpose(jnp.broadcast_to(lift_row, (LANES, chan)))
    for u in range(3):
        for v in range(3):
            at_v, at_u = slice(v * chan, (v + 1) * chan), slice(u * chan, (u + 1) * chan)
            wm1[at_v, at_u] = jnp.transpose(w4[u, v].astype(F32)).astype(BF16)
            wm2[at_v, at_u] = jnp.transpose(w8[u, v].astype(F32)).astype(BF16)
            wm3[at_v, at_u] = w8[2 - u, 2 - v]
    taps = []
    for v in range(3):
        taps.append(
            jnp.concatenate(
                [
                    jnp.sum(
                        w4[2 - u, 2 - v].astype(F32) * lift_col[:, :chan], axis=0, keepdims=True
                    )
                    for u in range(3)
                ],
                axis=1,
            )
        )
    tap_rows = jnp.concatenate(taps + [jnp.zeros((5, 3 * chan), F32)], axis=0)
    hi, mid, low_part = [p.astype(F32) for p in split(tap_rows, 3)]
    wm4[...] = jnp.concatenate(
        [hi, mid, low_part, jnp.zeros((8, 3 * chan), F32)], axis=0
    ).astype(BF16)

    each(1, tiles, lambda s: demand_copy(s).wait())
    total = dsend[pl.ds(pl.multiple_of(ti * rows, rows), in_rows), :].astype(F32)
    total = lax.fori_loop(1, tiles, lambda s, t: t + drecv[s].astype(F32), total)
    demand[...] = total

    for delta, k in order:
        if delta == 0:
            if k == 0:
                feat_copy(delta, k).wait()
            else:
                feat_copy(delta, k).wait_send()
                feat_arrival(delta, k).wait_recv()
        else:
            @pl.when((ti + delta >= 0) & (ti + delta < tiles))
            def _(delta=delta, k=k):
                feat_copy(delta, k).wait_send()

            @pl.when((ti - delta >= 0) & (ti - delta < tiles))
            def _(delta=delta, k=k):
                feat_arrival(delta, k).wait_recv()

    height = rows * tiles
    top = ti * rows

    def in_map(row):
        return (row >= 0) & (row < height)

    def fill(g, carry):
        at = g * GROUP
        ok = in_map(top - HALO + at)

        @pl.when(ok)
        def _():
            for j in range(GROUP):
                add = lift_col * demand[pl.ds(at + j, 1), :]
                inp[at + j] = (gath[at + j].astype(F32) + add).astype(BF16)

        @pl.when(jnp.logical_not(ok))
        def _():
            for j in range(GROUP):
                inp[at + j] = jnp.zeros((chan, LANES), BF16)

        return carry

    lax.fori_loop(0, in_rows // GROUP, fill, 0)

    col = lane + ci * own_cols - margin
    col_ok = ((col >= 0) & (col < cols)).astype(F32)

    def gathered(ref, at, dilation):
        return jnp.concatenate(
            [
                jnp.concatenate([ref[at + j + u * dilation] for u in range(3)], axis=0)
                for j in range(GROUP)
            ],
            axis=1,
        )

    def conv(ref, at, weights, dilation):
        result = jnp.dot(weights[...], gathered(ref, at, dilation), preferred_element_type=F32)
        parts = []
        for j in range(GROUP):
            one = result[:, j * LANES : (j + 1) * LANES]
            parts.append(
                one[chan : 2 * chan]
                + pltpu.roll(one[:chan], dilation, 1)
                + pltpu.roll(one[2 * chan :], LANES - dilation, 1)
            )
        return parts

    def keep_of(row):
        return col_ok * in_map(row).astype(F32)

    def first(g, carry):
        at = g * GROUP
        keep = keep_of(top - 20 + at)
        for j, value in enumerate(conv(inp, at, wm1, 4)):
            pre[at + j] = value
            hid[at + j] = (value * jax.nn.sigmoid(value) * keep).astype(BF16)
        return carry

    def second(g, carry):
        at = g * GROUP
        keep = keep_of(top - 12 + at)
        for j, value in enumerate(conv(hid, at, wm2, 8)):
            sec[at + j] = (jax.nn.sigmoid(value) * keep).astype(BF16)
        return carry

    def third(g, carry):
        at = g * GROUP
        keep = keep_of(top - 4 + at)
        for j, value in enumerate(conv(sec, at, wm3, 8)):
            p = pre[at + j + 16]
            s = jax.nn.sigmoid(p)
            gpre[at + j] = (value * s * (1.0 + p * (1.0 - s)) * keep).astype(BF16)
        return carry

    lax.fori_loop(0, (rows + 40) // GROUP, first, 0)
    lax.fori_loop(0, (rows + 24) // GROUP, second, 0)
    lax.fori_loop(0, (rows + 8) // GROUP, third, 0)

    owned = ((lane >= margin) & (lane < margin + own_cols)).astype(F32)
    for g in range(rows // GROUP):
        at = g * GROUP
        result = jnp.dot(wm4[...], gathered(gpre, at, 4), preferred_element_type=F32)
        result = result[0:8] + result[8:16] + result[16:24]
        for j in range(GROUP):
            one = result[:, j * LANES : (j + 1) * LANES]
            line = (
                one[1:2]
                + pltpu.roll(one, 4, 1)[0:1]
                + pltpu.roll(one, LANES - 4, 1)[2:3]
            )
            gown[at + j : at + j + 1, :] = line * owned

    def grad_copy(step):
        to = lax.rem(ti + step, tiles)
        return pltpu.make_async_remote_copy(
            src_ref=gown, dst_ref=gall.at[pl.ds(pl.multiple_of(ti * rows, rows), rows)],
            send_sem=gsend_sem.at[step], recv_sem=grecv_sem.at[step],
            device_id=(to, ci), device_id_type=MESH,
        )

    def grad_arrival(step):
        come = lax.rem(ti + tiles - step, tiles)
        dst = gall.at[pl.ds(pl.multiple_of(come * rows, rows), rows)]
        return pltpu.make_async_remote_copy(
            src_ref=gown, dst_ref=dst,
            send_sem=gsend_sem.at[step], recv_sem=grecv_sem.at[step],
            device_id=(lax.rem(ti + step, tiles), ci), device_id_type=MESH,
        )

    each(1, tiles, lambda s: grad_copy(s).start())
    mine = pltpu.make_async_copy(
        gown, gall.at[pl.ds(pl.multiple_of(ti * rows, rows), rows)], gown_sem
    )
    mine.start()
    map_blocks = height // TILE_ROWS
    block_lane = lax.broadcasted_iota(jnp.int32, (entries, map_blocks), 1).astype(F32)
    block_hot = jnp.where(columns[:, 0:1] == block_lane, 1.0, 0.0).astype(BF16)
    mine.wait()
    each(1, tiles, lambda s: grad_copy(s).wait_send())
    each(1, tiles, lambda s: grad_arrival(s).wait_recv())

    entry_sum = jnp.zeros((entries, LANES), F32)
    for i in range(TILE_ROWS):
        grads = gall[pl.ds(i, map_blocks, stride=TILE_ROWS), :]
        high, low_ = split(grads, 2)
        rows_of = jnp.dot(block_hot, high, preferred_element_type=F32)
        rows_of = rows_of + jnp.dot(block_hot, low_, preferred_element_type=F32)
        entry_sum = entry_sum + rows_of * fmask[:, i * LANES : (i + 1) * LANES].astype(F32)
    entry_grad = jnp.sum(entry_sum, axis=1, keepdims=True)
    pin_grad = jnp.sum(
        jnp.where(net_e_col == table[4:5, :], entry_grad, 0.0), axis=0, keepdims=True
    )
    dest_rows = max(8, tiles)
    dest_row = lax.broadcasted_iota(jnp.int32, (dest_rows, entries), 0).astype(F32)
    cell_row = lax.broadcasted_iota(jnp.int32, (LANES, entries), 0).astype(F32)
    by_dest = jnp.where(dest_row == table[5:6, :], pin_grad, 0.0)
    by_cell = jnp.where(cell_row == table[6:7, :], 1.0, 0.0).astype(BF16)
    pieces = jnp.concatenate([p.astype(F32) for p in split(by_dest, 3)], axis=0).astype(BF16)
    cells = lax.dot_general(
        pieces, by_cell, (((1,), (1,)), ((), ())), preferred_element_type=F32
    )
    cells = cells[:dest_rows] + cells[dest_rows : 2 * dest_rows] + cells[2 * dest_rows :]
    for t in range(tiles):
        csend[t] = cells[t : t + 1, :]

    def cell_copy(step):
        to = peer(step)
        return pltpu.make_async_remote_copy(
            src_ref=csend.at[to[0]], dst_ref=crecv.at[step],
            send_sem=csend_sem.at[step], recv_sem=crecv_sem.at[step],
            device_id=to, device_id_type=MESH,
        )

    each(1, others + 1, lambda s: cell_copy(s).start())
    each(1, others + 1, lambda s: cell_copy(s).wait())
    out[...] = lax.fori_loop(1, others + 1, lambda s, t: t + crecv[s], csend[ti])


def solution(mesh):
    tiles, chans = mesh.shape["tile"], mesh.shape["chan"]

    def local(
        feat, lift, w4, w8, frac, target, owner, net_e, weight, net_p, cell,
    ):
        rows, chan_own, cols = feat.shape
        chan = chan_own * chans
        entries = frac.shape[0]
        per_row = cols // TILE_COLS
        per_strip = rows // TILE_ROWS
        pack = jnp.stack(
            [
                (target[:, 0] * per_strip + owner // per_row).astype(F32),
                (owner % per_row).astype(F32),
                net_e.astype(F32),
                weight,
                net_p.astype(F32),
                (cell // CELL_DEV).astype(F32),
                (cell % CELL_DEV).astype(F32),
                jnp.zeros_like(weight),
            ]
        )
        in_rows = rows + 2 * HALO
        reach = -(-HALO // rows)
        height = rows * tiles
        blocks = -(-(height + 2 * HALO) // (8 * TILE_ROWS)) * 8
        vm = pltpu.VMEM
        dma = pltpu.SemaphoreType.DMA
        result = pl.pallas_call(
            functools.partial(kernel, tiles, chans),
            out_shape=jax.ShapeDtypeStruct((1, LANES), F32),
            in_specs=[pl.BlockSpec(memory_space=pltpu.VMEM)] * 6,
            out_specs=pl.BlockSpec(memory_space=pltpu.VMEM),
            scratch_shapes=[
                vm((chans, rows, chan_own, LANES), BF16),
                vm((in_rows, chan, LANES), BF16),
                vm((in_rows, chan, LANES), BF16),
                vm((rows + 40, chan, LANES), F32),
                vm((rows + 40, chan, LANES), BF16),
                vm((rows + 24, chan, LANES), BF16),
                vm((rows + 8, chan, LANES), BF16),
                vm((3 * chan, 3 * chan), BF16),
                vm((3 * chan, 3 * chan), BF16),
                vm((3 * chan, 3 * chan), BF16),
                vm((32, 3 * chan), BF16),
                vm((entries, TILE_ROWS * LANES), BF16),
                vm((blocks * TILE_ROWS, LANES), F32),
                vm((blocks * TILE_ROWS, LANES), BF16),
                vm((tiles, in_rows, LANES), BF16),
                vm((in_rows, LANES), F32),
                vm((rows, LANES), F32),
                vm((height, LANES), F32),
                vm((tiles, 1, LANES), F32),
                vm((tiles * chans, 1, LANES), F32),
                dma((2 * reach + 1, chans)),
                dma((2 * reach + 1, chans)),
                dma(()),
                dma((tiles,)),
                dma((tiles,)),
                dma((tiles,)),
                dma((tiles,)),
                dma(()),
                dma((tiles * chans,)),
                dma((tiles * chans,)),
            ],
            compiler_params=pltpu.CompilerParams(collective_id=0, has_side_effects=True),
        )(feat, lift.reshape(1, chan), w4, w8, frac, pack)
        return result[0, :CELL_DEV]

    in_specs = (
        P("tile", "chan", None), P(), P(), P(),
        P("tile", None), P("tile", None),
        P("tile"), P("tile"), P("tile"), P("tile"), P("tile"),
    )
    return jax.shard_map(
        local, mesh=mesh, in_specs=in_specs, out_specs=P("tile"), check_vma=False
    )
```

time: 196 us -> 49.5 us (0.25)
  waiting for transfers between devices: 57.2 us -> 0 us
  blocking collectives: 46 us -> 0 us
  Pallas kernels: 0 us -> 43.3 us
  starting transfers between devices: 42.2 us -> 0 us
  matrix products: 15.8 us -> 0 us
  between operations: 14.4 us -> 0.04 us
  other arithmetic: 11.8 us -> 0.03 us
    pallas_call x0 -> x1, Pallas kernels: none -> 43.3 us  [local(): pl.pallas_call(functools.partial(kernel, tiles, chans), out_shape=jax.Sha...]
    all_gather x2 -> x0, waiting for transfers between devices: 35.7 us -> none  [dilated_convolution(): lax.all_gather(rimmed, 'chan', axis=1, tiled=True)]
    ppermute x8 -> x0, starting transfers between devices: 23.8 us -> none  [the longest x4 18.7 us: extended(): before = lax.ppermute(last, axis, up)]
    all_to_all x3 -> x0, starting transfers between devices: 18.2 us -> none  [the longest x1 7.38 us: local(): lax.all_to_all(slot_grads.astype(jnp.bfloat16), 'tile', split_axis=0, con...]
    unnamed x1 -> x0, blocking collectives: 18.2 us -> none
    all_gather x2 -> x0, blocking collectives: 16.1 us -> none  [dilated_convolution(): lax.all_gather(rimmed, 'chan', axis=1, tiled=True)]
    dot_general x42 -> x0, matrix products: 15.8 us -> none  [the longest x36 12.4 us: dilated_convolution(): jnp.einsum('rcw,co->row', part_in, own_weights[row_tap, col_tap], preferr...]
    all_to_all x3 -> x0, waiting for transfers between devices: 14.5 us -> none  [the longest x1 6.09 us: local(): lax.all_to_all(slot_grads.astype(jnp.bfloat16), 'tile', split_axis=0, con...]
  transfers between devices with their start and end apart: 13 -> 0, of which waited for: 11 -> 0; matrix products, arithmetic and copies ran while one was open for 3% -> 0% of each run, Pallas kernels for 0% -> 0%
where the time goes in v1:
time: 49.5 us; the launch traced here: 49.2 us
  Pallas kernels  43.3 us (87%)
  local copies, waits for them, and re-layouts  5.85 us (12%)
    pallas_call x1, Pallas kernels, local(): pl.pallas_call(functools.partial(kernel, tiles, chans), out_shape=jax.Sha...  43.3 us
    unnamed x12, local copies, waits for them, and re-layouts  4.05 us
    squeeze x1, local copies, waits for them, and re-layouts, local(): return result[0, :CELL_DEV]  1.18 us

profile of v1, /device:TPU:0, one launch (start us, length us, event | category | flops | bytes accessed | tf_op | source)
XLA Modules:
  0.0 49.2 jit_solution(1108777813911794689)
XLA Ops:
  0.0 0.0 copy-start.2
  0.0 0.7 %copy-done.2 = s32[256,1]{0,1:T(1,128)S(1)} copy-done((s32[256,1]{0,1:T(1,128)S(1)}, s32[256,1]{0,1:T(1,128)}, u32[]{:S(2)}) %copy-start.2) | copy-done | bytes 1048
  0.7 0.0 copy-start.3
  0.7 0.7 %copy-done.3 = s32[256]{0:T(256)S(1)} copy-done((s32[256]{0:T(256)S(1)}, s32[256]{0:T(256)}, u32[]{:S(2)}) %copy-start.3) | copy-done | bytes 1048
  1.4 0.0 copy-start.4
  1.4 0.7 %copy-done.4 = s32[256]{0:T(256)S(1)} copy-done((s32[256]{0:T(256)S(1)}, s32[256]{0:T(256)}, u32[]{:S(2)}) %copy-start.4) | copy-done | bytes 1048
  2.0 0.0 copy-start.5
  2.1 0.7 %copy-done.5 = s32[256]{0:T(256)S(1)} copy-done((s32[256]{0:T(256)S(1)}, s32[256]{0:T(256)}, u32[]{:S(2)}) %copy-start.5) | copy-done | bytes 1048
  2.7 0.0 copy-start
  2.8 0.7 %copy-done = s32[256]{0:T(256)S(1)} copy-done((s32[256]{0:T(256)S(1)}, s32[256]{0:T(256)}, u32[]{:S(2)}) %copy-start) | copy-done | bytes 1048
  3.4 0.0 copy-start.1
  3.5 0.7 %copy-done.1 = f32[256]{0:T(256)S(1)} copy-done((f32[256]{0:T(256)S(1)}, f32[256]{0:T(256)}, u32[]{:S(2)}) %copy-start.1) | copy-done | bytes 1048
  4.1 0.6 %stack.31.pack = f32[8,256]{1,0:T(8,128)} concatenate(f32[1,256]{1,0:T(1,128)S(1)} %bitcast.16, f32[1,256]{1,0:T(1,128)S(1)} %bitcast.15, f32[1,256]{1,0:T(1,128)S(1)} %bitcast.13, f32[1,256]{1,0:T(1,128)S(1)} %bitcast.18, f32[1,256]{1,0:T(1,128)S(1)} %bitcast.14, f32[1,256]{1,0:T(1,128)S(1)} %bitcast.12, f32[1,256]{1,0:T(1,128)S(1)} %bitcast.11, f32[1,256]{1,0:T(1,128)S(1)} %stack_broadcast_in_dim.3), dimensions={0} | concatenate | bytes 16384 | tf_op jit(solution)/shard_map/stack | solution.py:372
  4.7 43.3 %shard_map.109 = f32[1,128]{1,0:T(1,128)} custom-call(bf16[16,16,256]{2,1,0:T(8,128)(2,1)} %feat.1, f32[1,64]{1,0:T(1,128)} %bitcast.19, bf16[3,3,64,64]{3,2,1,0:T(8,128)(2,1)} %w4.1, bf16[3,3,64,64]{3,2,1,0:T(8,128)(2,1)} %w8.1, bf16[256,128]{1,0:T(8,128)(2,1)} %frac.1, f32[8,256]{1,0:T(8,128)} %stack.31.pack), custom_call_target="tpu_custom_call" | custom-call | tf_op jit(solution)/shard_map/pallas_call | solution.py:390
  48.1 1.2 %slice_bitcast_fusion = f32[64]{0:T(128)} fusion(f32[1,128]{1,0:T(1,128)} %shard_map.109), kind=kLoop, calls=%fused_computation.15 | loop fusion | bytes 512 | tf_op jit(solution)/shard_map/squeeze | solution.py:429
  (6 shorter events, 0.0 us)
Async XLA Ops:
  0.0 0.7 %copy-start.2 = (s32[256,1]{0,1:T(1,128)S(1)}, s32[256,1]{0,1:T(1,128)}, u32[]{:S(2)}) copy-start(s32[256,1]{0,1:T(1,128)} %param.16) | copy-start | bytes 3076
  0.7 0.7 %copy-start.3 = (s32[256]{0:T(256)S(1)}, s32[256]{0:T(256)}, u32[]{:S(2)}) copy-start(s32[256]{0:T(256)} %param.18) | copy-start | bytes 3076
  1.4 0.7 %copy-start.4 = (s32[256]{0:T(256)S(1)}, s32[256]{0:T(256)}, u32[]{:S(2)}) copy-start(s32[256]{0:T(256)} %param.20) | copy-start | bytes 3076
  2.0 0.7 %copy-start.5 = (s32[256]{0:T(256)S(1)}, s32[256]{0:T(256)}, u32[]{:S(2)}) copy-start(s32[256]{0:T(256)} %param.17) | copy-start | bytes 3076
  2.7 0.7 %copy-start = (s32[256]{0:T(256)S(1)}, s32[256]{0:T(256)}, u32[]{:S(2)}) copy-start(s32[256]{0:T(256)} %param.21) | copy-start | bytes 3076
  3.4 0.7 %copy-start.1 = (f32[256]{0:T(256)S(1)}, f32[256]{0:T(256)}, u32[]{:S(2)}) copy-start(f32[256]{0:T(256)} %param.19) | copy-start | bytes 3076

commit v2 on v1

--- a/solution.py
+++ b/solution.py
@@ -29,8 +29,10 @@
 
 def kernel(
     tiles, chans,
-    feat, lift, w4, w8, frac, pack,
+    feat_in, lift_in, w4_in, w8_in, frac_in, target_in, owner_in, net_e_in, weight_in, net_p_in,
+    cell_in,
     out,
+    feat, lift, w4, w8, frac, target, owner, net_e, weight, net_p, cell, load_sem,
     win, gath, inp, pre, hid, sec, gpre, wm1, wm2, wm3, wm4,
     fmask, dbuf, dsend, drecv, demand, gown, gall, csend, crecv,
     fsend_sem, frecv_sem, own_sem, dsend_sem, drecv_sem, gsend_sem, grecv_sem, gown_sem,
@@ -46,6 +48,19 @@
     in_rows = rows + 2 * HALO
     others = tiles * chans - 1
 
+    loads = [
+        pltpu.make_async_copy(src, dst, load_sem.at[n])
+        for n, (src, dst) in enumerate(
+            [
+                (feat_in, feat), (target_in, target), (owner_in, owner), (net_e_in, net_e),
+                (weight_in, weight), (net_p_in, net_p), (frac_in, frac), (lift_in, lift),
+                (cell_in, cell), (w4_in, w4), (w8_in, w8),
+            ]
+        )
+    ]
+    for load in loads:
+        load.start()
+
     barrier = pltpu.get_barrier_semaphore()
 
     def peer(step):
@@ -57,6 +72,8 @@
         return carry
 
     lax.fori_loop(1, others + 1, greet, 0)
+
+    loads[0].wait()
 
     flat = feat[...].astype(F32).reshape(rows * chan_own, cols)
     lane = lax.broadcasted_iota(jnp.int32, (1, LANES), 1)
@@ -106,7 +123,23 @@
             def _(delta=delta, k=k):
                 feat_copy(delta, k).start()
 
-    table = pack[...]
+    for load in loads[1:]:
+        load.wait()
+    per_row = cols // TILE_COLS
+    own, cell_no = owner[...], cell[...]
+    table = jnp.concatenate(
+        [
+            (target[...] * (rows // TILE_ROWS) + own // per_row).astype(F32),
+            (own % per_row).astype(F32),
+            net_e[...].astype(F32),
+            weight[...],
+            net_p[...].astype(F32),
+            (cell_no // CELL_DEV).astype(F32),
+            (cell_no % CELL_DEV).astype(F32),
+            jnp.zeros_like(weight[...]),
+        ],
+        axis=0,
+    )
     columns = jnp.transpose(table)
     entries = table.shape[1]
     net_e_col, wpin_col, net_p_col = columns[:, 2:3], columns[:, 3:4], columns[:, 4:5]
@@ -367,20 +400,7 @@
         rows, chan_own, cols = feat.shape
         chan = chan_own * chans
         entries = frac.shape[0]
-        per_row = cols // TILE_COLS
-        per_strip = rows // TILE_ROWS
-        pack = jnp.stack(
-            [
-                (target[:, 0] * per_strip + owner // per_row).astype(F32),
-                (owner % per_row).astype(F32),
-                net_e.astype(F32),
-                weight,
-                net_p.astype(F32),
-                (cell // CELL_DEV).astype(F32),
-                (cell % CELL_DEV).astype(F32),
-                jnp.zeros_like(weight),
-            ]
-        )
+        pins = weight.shape[0]
         in_rows = rows + 2 * HALO
         reach = -(-HALO // rows)
         height = rows * tiles
@@ -390,9 +410,21 @@
         result = pl.pallas_call(
             functools.partial(kernel, tiles, chans),
             out_shape=jax.ShapeDtypeStruct((1, LANES), F32),
-            in_specs=[pl.BlockSpec(memory_space=pltpu.VMEM)] * 6,
+            in_specs=[pl.BlockSpec(memory_space=pltpu.HBM)] * 11,
             out_specs=pl.BlockSpec(memory_space=pltpu.VMEM),
             scratch_shapes=[
+                vm(feat.shape, BF16),
+                vm((1, chan), F32),
+                vm(w4.shape, BF16),
+                vm(w8.shape, BF16),
+                vm(frac.shape, BF16),
+                vm((1, entries), jnp.int32),
+                vm((1, entries), jnp.int32),
+                vm((1, entries), jnp.int32),
+                vm((1, pins), F32),
+                vm((1, pins), jnp.int32),
+                vm((1, pins), jnp.int32),
+                dma((11,)),
                 vm((chans, rows, chan_own, LANES), BF16),
                 vm((in_rows, chan, LANES), BF16),
                 vm((in_rows, chan, LANES), BF16),
@@ -425,7 +457,11 @@
                 dma((tiles * chans,)),
             ],
             compiler_params=pltpu.CompilerParams(collective_id=0, has_side_effects=True),
-        )(feat, lift.reshape(1, chan), w4, w8, frac, pack)
+        )(
+            feat, lift.reshape(1, chan), w4, w8, frac, target.reshape(1, entries),
+            owner.reshape(1, entries), net_e.reshape(1, entries), weight.reshape(1, pins),
+            net_p.reshape(1, pins), cell.reshape(1, pins),
+        )
         return result[0, :CELL_DEV]
 
     in_specs = (

time: 49.5 us -> 43.8 us (0.88)
  local copies, waits for them, and re-layouts: 5.85 us -> 1.19 us
  Pallas kernels: 43.3 us -> 42.4 us
    unnamed x12 -> x0, local copies, waits for them, and re-layouts: 4.05 us -> none
    pallas_call x1, Pallas kernels: 43.3 us -> 42.4 us  [local(): pl.pallas_call(functools.partial(kernel, tiles, chans), out_shape=jax.Sha...]
    another operation x2 -> x0, local copies, waits for them, and re-layouts: 0.62 us -> none  [local(): jnp.stack([(target[:, 0] * per_strip + owner // per_row).astype(F32), (ow...]
where the time goes in v2:
time: 43.8 us; the launch traced here: 43.6 us
  Pallas kernels  42.4 us (97%)
  local copies, waits for them, and re-layouts  1.19 us (3%)
    pallas_call x1, Pallas kernels, local(): pl.pallas_call(functools.partial(kernel, tiles, chans), out_shape=jax.Sha...  42.4 us
    squeeze x1, local copies, waits for them, and re-layouts, local(): return result[0, :CELL_DEV]  1.19 us

profile of v2, /device:TPU:0, one launch (start us, length us, event | category | flops | bytes accessed | tf_op | source)
XLA Modules:
  0.0 43.6 jit_solution(4868122845521179910)
XLA Ops:
  0.0 42.4 %shard_map.109 = f32[1,128]{1,0:T(1,128)} custom-call(bf16[16,16,256]{2,1,0:T(8,128)(2,1)} %feat_in.1, f32[1,64]{1,0:T(1,128)} %bitcast.15, bf16[3,3,64,64]{3,2,1,0:T(8,128)(2,1)} %w4_in.1, bf16[3,3,64,64]{3,2,1,0:T(8,128)(2,1)} %w8_in.1, bf16[256,128]{1,0:T(8,128)(2,1)} %frac_in.1, s32[1,256]{1,0:T(1,128)} %bitcast.9, s32[1,256]{1,0:T(1,128)} %bitcast.10, ...), custom_call_target="tpu_custom_call" | custom-call | tf_op jit(solution)/shard_map/pallas_call | solution.py:410
  42.4 1.2 %slice_bitcast_fusion = f32[64]{0:T(128)} fusion(f32[1,128]{1,0:T(1,128)} %shard_map.109), kind=kLoop, calls=%fused_computation | loop fusion | bytes 512 | tf_op jit(solution)/shard_map/squeeze | solution.py:465

commit v3 on v2

--- a/solution.py
+++ b/solution.py
@@ -34,7 +34,7 @@
     out,
     feat, lift, w4, w8, frac, target, owner, net_e, weight, net_p, cell, load_sem,
     win, gath, inp, pre, hid, sec, gpre, wm1, wm2, wm3, wm4,
-    fmask, dbuf, dsend, drecv, demand, gown, gall, csend, crecv,
+    fmask, block_hot, same_net, by_dest, by_cell, dbuf, dsend, drecv, demand, gown, gall, csend, crecv,
     fsend_sem, frecv_sem, own_sem, dsend_sem, drecv_sem, gsend_sem, grecv_sem, gown_sem,
     csend_sem, crecv_sem,
 ):
@@ -63,15 +63,31 @@
 
     barrier = pltpu.get_barrier_semaphore()
 
-    def peer(step):
-        number = lax.rem(ti * chans + ci + step, tiles * chans)
-        return lax.div(number, chans), lax.rem(number, chans)
-
-    def greet(step, carry):
-        pl.semaphore_signal(barrier, inc=1, device_id=peer(step), device_id_type=MESH)
-        return carry
-
-    lax.fori_loop(1, others + 1, greet, 0)
+    def wrap(number, count):
+        return jnp.where(number >= count, number - count, number)
+
+    def each(lo, hi, fn):
+        if hi - lo <= 32:
+            for step in range(lo, hi):
+                fn(step)
+        else:
+            def body(step, carry):
+                fn(step)
+                return carry
+            lax.fori_loop(lo, hi, body, 0)
+
+    def each_peer(fn):
+        def along(back):
+            hop = tiles - 1 - back
+            for turn in range(chans):
+                fn(hop * chans + turn, (wrap(ti + hop, tiles), wrap(ci + turn, chans)))
+        each(0, tiles - 1, along)
+        for turn in range(1, chans):
+            fn(turn, (ti, wrap(ci + turn, chans)))
+
+    each_peer(
+        lambda n, who: pl.semaphore_signal(barrier, inc=1, device_id=who, device_id_type=MESH)
+    )
 
     loads[0].wait()
 
@@ -93,7 +109,7 @@
 
     def feat_copy(delta, k):
         low, count, at = spans(delta)
-        to = lax.rem(ci + k, chans)
+        to = wrap(ci + k, chans)
         src = win.at[to, pl.ds(low, count)]
         dst = gath.at[pl.ds(at, count), pl.ds(pl.multiple_of(ci * chan_own, chan_own), chan_own)]
         if delta == 0 and k == 0:
@@ -106,22 +122,29 @@
 
     def feat_arrival(delta, k):
         low, count, at = spans(delta)
-        come = lax.rem(ci + chans - k, chans)
+        come = wrap(ci + chans - k, chans)
         dst = gath.at[pl.ds(at, count), pl.ds(pl.multiple_of(come * chan_own, chan_own), chan_own)]
         return pltpu.make_async_remote_copy(
             src_ref=dst, dst_ref=dst,
             send_sem=fsend_sem.at[delta + reach, k], recv_sem=frecv_sem.at[delta + reach, k],
-            device_id=(ti, lax.rem(ci + 1, chans)), device_id_type=MESH,
-        )
-
-    order = [(d, k) for d in sorted(range(-reach, reach + 1), key=lambda d: -abs(d)) for k in range(chans)]
-    for delta, k in order:
-        if delta == 0:
-            feat_copy(delta, k).start()
-        else:
-            @pl.when((ti + delta >= 0) & (ti + delta < tiles))
-            def _(delta=delta, k=k):
+            device_id=(ti, wrap(ci + 1, chans)), device_id_type=MESH,
+        )
+
+    stages = [[0]] + [[d] if abs(d) == 1 else [d, -d] for d in (1, -1, *range(2, reach + 1))]
+    for delta in sum(stages, []):
+        for k in range(chans):
+            if delta == 0:
                 feat_copy(delta, k).start()
+            else:
+                @pl.when((ti + delta >= 0) & (ti + delta < tiles))
+                def _(delta=delta, k=k):
+                    feat_copy(delta, k).start()
+
+    for delta in sum(stages[1:], []):
+        @pl.when((ti - delta < 0) | (ti - delta >= tiles))
+        def _(delta=delta):
+            low, count, at = spans(delta)
+            gath[at : at + count] = jnp.zeros((count, chan, LANES), BF16)
 
     for load in loads[1:]:
         load.wait()
@@ -167,19 +190,13 @@
     dsend[...] = dbuf[...].astype(BF16)
 
     def demand_copy(step):
-        to = lax.rem(ti + step, tiles)
+        to = wrap(ti + step, tiles)
         return pltpu.make_async_remote_copy(
             src_ref=dsend.at[pl.ds(pl.multiple_of(to * rows, rows), in_rows)],
             dst_ref=drecv.at[step],
             send_sem=dsend_sem.at[step], recv_sem=drecv_sem.at[step],
             device_id=(to, ci), device_id_type=MESH,
         )
-
-    def each(lo, hi, fn):
-        def body(step, carry):
-            fn(step)
-            return carry
-        lax.fori_loop(lo, hi, body, 0)
 
     each(1, tiles, lambda s: demand_copy(s).start())
 
@@ -210,26 +227,31 @@
         [hi, mid, low_part, jnp.zeros((8, 3 * chan), F32)], axis=0
     ).astype(BF16)
 
+    map_blocks = rows * tiles // TILE_ROWS
+    block_lane = lax.broadcasted_iota(jnp.int32, (entries, map_blocks), 1).astype(F32)
+    block_hot[...] = jnp.where(columns[:, 0:1] == block_lane, 1.0, 0.0).astype(BF16)
+    same_net[...] = jnp.where(net_e_col == table[4:5, :], 1.0, 0.0)
+    dest_rows = max(8, tiles)
+    dest_row = lax.broadcasted_iota(jnp.int32, (dest_rows, entries), 0).astype(F32)
+    cell_row = lax.broadcasted_iota(jnp.int32, (LANES, entries), 0).astype(F32)
+    by_dest[...] = jnp.where(dest_row == table[5:6, :], 1.0, 0.0)
+    by_cell[...] = jnp.where(cell_row == table[6:7, :], 1.0, 0.0).astype(BF16)
+
     each(1, tiles, lambda s: demand_copy(s).wait())
     total = dsend[pl.ds(pl.multiple_of(ti * rows, rows), in_rows), :].astype(F32)
     total = lax.fori_loop(1, tiles, lambda s, t: t + drecv[s].astype(F32), total)
     demand[...] = total
 
-    for delta, k in order:
+    def feat_wait(delta):
         if delta == 0:
-            if k == 0:
-                feat_copy(delta, k).wait()
-            else:
-                feat_copy(delta, k).wait_send()
+            feat_copy(delta, 0).wait()
+            for k in range(1, chans):
                 feat_arrival(delta, k).wait_recv()
         else:
-            @pl.when((ti + delta >= 0) & (ti + delta < tiles))
-            def _(delta=delta, k=k):
-                feat_copy(delta, k).wait_send()
-
             @pl.when((ti - delta >= 0) & (ti - delta < tiles))
-            def _(delta=delta, k=k):
-                feat_arrival(delta, k).wait_recv()
+            def _():
+                for k in range(chans):
+                    feat_arrival(delta, k).wait_recv()
 
     height = rows * tiles
     top = ti * rows
@@ -237,24 +259,10 @@
     def in_map(row):
         return (row >= 0) & (row < height)
 
-    def fill(g, carry):
-        at = g * GROUP
-        ok = in_map(top - HALO + at)
-
-        @pl.when(ok)
-        def _():
-            for j in range(GROUP):
-                add = lift_col * demand[pl.ds(at + j, 1), :]
-                inp[at + j] = (gath[at + j].astype(F32) + add).astype(BF16)
-
-        @pl.when(jnp.logical_not(ok))
-        def _():
-            for j in range(GROUP):
-                inp[at + j] = jnp.zeros((chan, LANES), BF16)
-
-        return carry
-
-    lax.fori_loop(0, in_rows // GROUP, fill, 0)
+    def fill(at):
+        for j in range(at, at + GROUP):
+            add = lift_col * demand[j : j + 1, :]
+            inp[j] = (gath[j].astype(F32) + add).astype(BF16)
 
     col = lane + ci * own_cols - margin
     col_ok = ((col >= 0) & (col < cols)).astype(F32)
@@ -283,33 +291,43 @@
     def keep_of(row):
         return col_ok * in_map(row).astype(F32)
 
-    def first(g, carry):
-        at = g * GROUP
+    def first(at):
         keep = keep_of(top - 20 + at)
         for j, value in enumerate(conv(inp, at, wm1, 4)):
             pre[at + j] = value
             hid[at + j] = (value * jax.nn.sigmoid(value) * keep).astype(BF16)
-        return carry
-
-    def second(g, carry):
-        at = g * GROUP
+
+    def second(at):
         keep = keep_of(top - 12 + at)
         for j, value in enumerate(conv(hid, at, wm2, 8)):
             sec[at + j] = (jax.nn.sigmoid(value) * keep).astype(BF16)
-        return carry
-
-    def third(g, carry):
-        at = g * GROUP
+
+    def third(at):
         keep = keep_of(top - 4 + at)
         for j, value in enumerate(conv(sec, at, wm3, 8)):
             p = pre[at + j + 16]
             s = jax.nn.sigmoid(p)
             gpre[at + j] = (value * s * (1.0 + p * (1.0 - s)) * keep).astype(BF16)
-        return carry
-
-    lax.fori_loop(0, (rows + 40) // GROUP, first, 0)
-    lax.fori_loop(0, (rows + 24) // GROUP, second, 0)
-    lax.fori_loop(0, (rows + 8) // GROUP, third, 0)
+
+    here, done = set(), set()
+    for stage in stages:
+        fresh = set()
+        for delta in stage:
+            feat_wait(delta)
+            low, count, at = spans(delta)
+            fresh |= set(range(at, at + count))
+        here |= fresh
+        for at in range(0, in_rows, GROUP):
+            if at in fresh:
+                fill(at)
+        for at in range(0, rows + 40, GROUP):
+            if at not in done and all(at + j in here for j in range(GROUP + 8)):
+                done.add(at)
+                first(at)
+    for at in range(0, rows + 24, GROUP):
+        second(at)
+    for at in range(0, rows + 8, GROUP):
+        third(at)
 
     owned = ((lane >= margin) & (lane < margin + own_cols)).astype(F32)
     for g in range(rows // GROUP):
@@ -326,7 +344,7 @@
             gown[at + j : at + j + 1, :] = line * owned
 
     def grad_copy(step):
-        to = lax.rem(ti + step, tiles)
+        to = wrap(ti + step, tiles)
         return pltpu.make_async_remote_copy(
             src_ref=gown, dst_ref=gall.at[pl.ds(pl.multiple_of(ti * rows, rows), rows)],
             send_sem=gsend_sem.at[step], recv_sem=grecv_sem.at[step],
@@ -334,12 +352,12 @@
         )
 
     def grad_arrival(step):
-        come = lax.rem(ti + tiles - step, tiles)
+        come = wrap(ti + tiles - step, tiles)
         dst = gall.at[pl.ds(pl.multiple_of(come * rows, rows), rows)]
         return pltpu.make_async_remote_copy(
             src_ref=gown, dst_ref=dst,
             send_sem=gsend_sem.at[step], recv_sem=grecv_sem.at[step],
-            device_id=(lax.rem(ti + step, tiles), ci), device_id_type=MESH,
+            device_id=(wrap(ti + step, tiles), ci), device_id_type=MESH,
         )
 
     each(1, tiles, lambda s: grad_copy(s).start())
@@ -347,48 +365,51 @@
         gown, gall.at[pl.ds(pl.multiple_of(ti * rows, rows), rows)], gown_sem
     )
     mine.start()
-    map_blocks = height // TILE_ROWS
-    block_lane = lax.broadcasted_iota(jnp.int32, (entries, map_blocks), 1).astype(F32)
-    block_hot = jnp.where(columns[:, 0:1] == block_lane, 1.0, 0.0).astype(BF16)
     mine.wait()
-    each(1, tiles, lambda s: grad_copy(s).wait_send())
     each(1, tiles, lambda s: grad_arrival(s).wait_recv())
 
     entry_sum = jnp.zeros((entries, LANES), F32)
     for i in range(TILE_ROWS):
         grads = gall[pl.ds(i, map_blocks, stride=TILE_ROWS), :]
         high, low_ = split(grads, 2)
-        rows_of = jnp.dot(block_hot, high, preferred_element_type=F32)
-        rows_of = rows_of + jnp.dot(block_hot, low_, preferred_element_type=F32)
+        rows_of = jnp.dot(block_hot[...], high, preferred_element_type=F32)
+        rows_of = rows_of + jnp.dot(block_hot[...], low_, preferred_element_type=F32)
         entry_sum = entry_sum + rows_of * fmask[:, i * LANES : (i + 1) * LANES].astype(F32)
     entry_grad = jnp.sum(entry_sum, axis=1, keepdims=True)
-    pin_grad = jnp.sum(
-        jnp.where(net_e_col == table[4:5, :], entry_grad, 0.0), axis=0, keepdims=True
-    )
-    dest_rows = max(8, tiles)
-    dest_row = lax.broadcasted_iota(jnp.int32, (dest_rows, entries), 0).astype(F32)
-    cell_row = lax.broadcasted_iota(jnp.int32, (LANES, entries), 0).astype(F32)
-    by_dest = jnp.where(dest_row == table[5:6, :], pin_grad, 0.0)
-    by_cell = jnp.where(cell_row == table[6:7, :], 1.0, 0.0).astype(BF16)
-    pieces = jnp.concatenate([p.astype(F32) for p in split(by_dest, 3)], axis=0).astype(BF16)
+    pin_grad = jnp.sum(same_net[...] * entry_grad, axis=0, keepdims=True)
+    pieces = jnp.concatenate([p.astype(F32) for p in split(by_dest[...] * pin_grad, 3)], axis=0).astype(BF16)
     cells = lax.dot_general(
-        pieces, by_cell, (((1,), (1,)), ((), ())), preferred_element_type=F32
+        pieces, by_cell[...], (((1,), (1,)), ((), ())), preferred_element_type=F32
     )
     cells = cells[:dest_rows] + cells[dest_rows : 2 * dest_rows] + cells[2 * dest_rows :]
     for t in range(tiles):
         csend[t] = cells[t : t + 1, :]
 
-    def cell_copy(step):
-        to = peer(step)
+    def cell_copy(step, to):
         return pltpu.make_async_remote_copy(
             src_ref=csend.at[to[0]], dst_ref=crecv.at[step],
-            send_sem=csend_sem.at[step], recv_sem=crecv_sem.at[step],
+            send_sem=csend_sem, recv_sem=crecv_sem,
             device_id=to, device_id_type=MESH,
         )
 
-    each(1, others + 1, lambda s: cell_copy(s).start())
-    each(1, others + 1, lambda s: cell_copy(s).wait())
-    out[...] = lax.fori_loop(1, others + 1, lambda s, t: t + crecv[s], csend[ti])
+    each_peer(lambda n, who: cell_copy(n, who).start())
+
+    for delta in sum(stages, []):
+        for k in range(chans):
+            if delta == 0:
+                if k:
+                    feat_copy(delta, k).wait_send()
+            else:
+                @pl.when((ti + delta >= 0) & (ti + delta < tiles))
+                def _(delta=delta, k=k):
+                    feat_copy(delta, k).wait_send()
+    each(1, tiles, lambda s: grad_copy(s).wait_send())
+    arrived = crecv.at[pl.ds(1, others)]
+    pltpu.make_async_remote_copy(
+        src_ref=arrived, dst_ref=arrived, send_sem=csend_sem, recv_sem=crecv_sem,
+        device_id=(ti, wrap(ci + 1, chans)), device_id_type=MESH,
+    ).wait()
+    out[...] = csend[ti] + jnp.sum(crecv[1:], axis=0)
 
 
 def solution(mesh):
@@ -437,6 +458,10 @@
                 vm((3 * chan, 3 * chan), BF16),
                 vm((32, 3 * chan), BF16),
                 vm((entries, TILE_ROWS * LANES), BF16),
+                vm((entries, height // TILE_ROWS), BF16),
+                vm((entries, pins), F32),
+                vm((max(8, tiles), pins), F32),
+                vm((LANES, pins), BF16),
                 vm((blocks * TILE_ROWS, LANES), F32),
                 vm((blocks * TILE_ROWS, LANES), BF16),
                 vm((tiles, in_rows, LANES), BF16),
@@ -453,8 +478,8 @@
                 dma((tiles,)),
                 dma((tiles,)),
                 dma(()),
-                dma((tiles * chans,)),
-                dma((tiles * chans,)),
+                dma(()),
+                dma(()),
             ],
             compiler_params=pltpu.CompilerParams(collective_id=0, has_side_effects=True),
         )(

time: 43.8 us -> 36.8 us (0.84)
  Pallas kernels: 42.4 us -> 35.4 us
    pallas_call x1, Pallas kernels: 42.4 us -> 35.4 us  [local(): pl.pallas_call(functools.partial(kernel, tiles, chans), out_shape=jax.Sha...]
where the time goes in v3:
time: 36.8 us; the launch traced here: 36.6 us
  Pallas kernels  35.4 us (96%)
  local copies, waits for them, and re-layouts  1.19 us (3%)
    pallas_call x1, Pallas kernels, local(): pl.pallas_call(functools.partial(kernel, tiles, chans), out_shape=jax.Sha...  35.4 us
    squeeze x1, local copies, waits for them, and re-layouts, local(): return result[0, :CELL_DEV]  1.19 us

profile of v3, /device:TPU:0, one launch (start us, length us, event | category | flops | bytes accessed | tf_op | source)
XLA Modules:
  0.0 36.6 jit_solution(18106425719247921067)
XLA Ops:
  0.0 35.4 %shard_map.109 = f32[1,128]{1,0:T(1,128)} custom-call(bf16[16,16,256]{2,1,0:T(8,128)(2,1)} %feat_in.1, f32[1,64]{1,0:T(1,128)} %bitcast.15, bf16[3,3,64,64]{3,2,1,0:T(8,128)(2,1)} %w4_in.1, bf16[3,3,64,64]{3,2,1,0:T(8,128)(2,1)} %w8_in.1, bf16[256,128]{1,0:T(8,128)(2,1)} %frac_in.1, s32[1,256]{1,0:T(1,128)} %bitcast.9, s32[1,256]{1,0:T(1,128)} %bitcast.10, ...), custom_call_target="tpu_custom_call" | custom-call | tf_op jit(solution)/shard_map/pallas_call | solution.py:431
  35.5 1.2 %slice_bitcast_fusion = f32[64]{0:T(128)} fusion(f32[1,128]{1,0:T(1,128)} %shard_map.109), kind=kLoop, calls=%fused_computation | loop fusion | bytes 512 | tf_op jit(solution)/shard_map/squeeze | solution.py:490

commit v4 on v3

--- a/solution.py
+++ b/solution.py
@@ -99,8 +99,6 @@
         inside = (lane + first >= 0) & (lane + first < cols)
         win[k] = jnp.where(inside, turned, 0.0).astype(BF16).reshape(rows, chan_own, LANES)
 
-    pl.semaphore_wait(barrier, others)
-
     def spans(delta):
         start = HALO - rows * delta
         low = max(0, -start)
@@ -131,15 +129,6 @@
         )
 
     stages = [[0]] + [[d] if abs(d) == 1 else [d, -d] for d in (1, -1, *range(2, reach + 1))]
-    for delta in sum(stages, []):
-        for k in range(chans):
-            if delta == 0:
-                feat_copy(delta, k).start()
-            else:
-                @pl.when((ti + delta >= 0) & (ti + delta < tiles))
-                def _(delta=delta, k=k):
-                    feat_copy(delta, k).start()
-
     for delta in sum(stages[1:], []):
         @pl.when((ti - delta < 0) | (ti - delta >= tiles))
         def _(delta=delta):
@@ -197,8 +186,6 @@
             send_sem=dsend_sem.at[step], recv_sem=drecv_sem.at[step],
             device_id=(to, ci), device_id_type=MESH,
         )
-
-    each(1, tiles, lambda s: demand_copy(s).start())
 
     lift_row = lift[...]
     lift_col = jnp.transpose(jnp.broadcast_to(lift_row, (LANES, chan)))
@@ -236,6 +223,19 @@
     cell_row = lax.broadcasted_iota(jnp.int32, (LANES, entries), 0).astype(F32)
     by_dest[...] = jnp.where(dest_row == table[5:6, :], 1.0, 0.0)
     by_cell[...] = jnp.where(cell_row == table[6:7, :], 1.0, 0.0).astype(BF16)
+
+    pl.semaphore_wait(barrier, others)
+
+    each(1, tiles, lambda s: demand_copy(s).start())
+
+    for delta in sum(stages, []):
+        for k in range(chans):
+            if delta == 0:
+                feat_copy(delta, k).start()
+            else:
+                @pl.when((ti + delta >= 0) & (ti + delta < tiles))
+                def _(delta=delta, k=k):
+                    feat_copy(delta, k).start()
 
     each(1, tiles, lambda s: demand_copy(s).wait())
     total = dsend[pl.ds(pl.multiple_of(ti * rows, rows), in_rows), :].astype(F32)

time: 36.8 us -> 36 us (0.978)
  Pallas kernels: 35.4 us -> 34.7 us
    pallas_call x1, Pallas kernels: 35.4 us -> 34.7 us  [local(): pl.pallas_call(functools.partial(kernel, tiles, chans), out_shape=jax.Sha...]
where the time goes in v4:
time: 36 us; the launch traced here: 35.9 us
  Pallas kernels  34.7 us (96%)
  local copies, waits for them, and re-layouts  1.19 us (3%)
    pallas_call x1, Pallas kernels, local(): pl.pallas_call(functools.partial(kernel, tiles, chans), out_shape=jax.Sha...  34.7 us
    squeeze x1, local copies, waits for them, and re-layouts, local(): return result[0, :CELL_DEV]  1.19 us

profile of v4, /device:TPU:0, one launch (start us, length us, event | category | flops | bytes accessed | tf_op | source)
XLA Modules:
  0.0 35.9 jit_solution(2307954516210022291)
XLA Ops:
  0.0 34.7 %shard_map.109 = f32[1,128]{1,0:T(1,128)} custom-call(bf16[16,16,256]{2,1,0:T(8,128)(2,1)} %feat_in.1, f32[1,64]{1,0:T(1,128)} %bitcast.15, bf16[3,3,64,64]{3,2,1,0:T(8,128)(2,1)} %w4_in.1, bf16[3,3,64,64]{3,2,1,0:T(8,128)(2,1)} %w8_in.1, bf16[256,128]{1,0:T(8,128)(2,1)} %frac_in.1, s32[1,256]{1,0:T(1,128)} %bitcast.9, s32[1,256]{1,0:T(1,128)} %bitcast.10, ...), custom_call_target="tpu_custom_call" | custom-call | tf_op jit(solution)/shard_map/pallas_call | solution.py:431
  34.7 1.2 %slice_bitcast_fusion = f32[64]{0:T(128)} fusion(f32[1,128]{1,0:T(1,128)} %shard_map.109), kind=kLoop, calls=%fused_computation | loop fusion | bytes 512 | tf_op jit(solution)/shard_map/squeeze | solution.py:490
